TPU v7x, 128 devices: a whole 4x4x4 slice. The times are simulated.
128 devices in a mesh: frames: 2 (over y_hi), codebook: 16 (over y_lo, x, core), hidden: 4 (over z).
Axes of the slice: x: 4, y: 4 (y_hi: 2, y_lo: 2; y = y_hi * 2 + y_lo), z: 4, core: 2. Of those that a mesh axis runs over, the one named last changes fastest.
Arguments:
- temporal: bfloat16 [4096, 4096], P(('frames', 'codebook'), 'hidden'), may hold values from -6 to 6
- frame_ids: int32 [4096, 16], P('frames', 'codebook'), may hold values from 0 to 2047
- proj_weight: bfloat16 [16, 4096, 1024], P('codebook', 'hidden'), may hold values from -0.09375 to 0.09375
- embed_table: bfloat16 [16, 2049, 1024], P('codebook'), may hold values from -6 to 6
- qkv_weight: bfloat16 [16, 3, 1024, 1024], P('codebook', None, None, 'hidden'), may hold values from -12 to 12
- out_weight: bfloat16 [16, 1024, 1024], P('codebook', 'hidden'), may hold values from -0.1875 to 0.1875
- gate_up: bfloat16 [16, 2, 1024, 4096], P('codebook', None, None, 'hidden'), may hold values from -0.1875 to 0.1875
- down_weight: bfloat16 [16, 4096, 1024], P('codebook', 'hidden'), may hold values from -0.09375 to 0.09375
- norm_gains: float32 [16, 2, 1024], P('codebook'), may hold values from 0.25 to 1.75
Outputs:
- depth_states: float32 [16, 4096, 1024], P('codebook', 'frames', 'hidden')
All inputs are finite; a program needn't handle non-finite values.
Results may differ from a plain program's by a relative error of at most 0.015.
Values may be sent and summed in bfloat16 or wider, within the bound.
A program may use at most 192 MiB of HBM per device.

v0:
```python
import jax
import jax.numpy as jnp
from jax import lax
from jax.sharding import PartitionSpec as P

HEADS = 16


def shifted(block, axis, distance):
    devices = range(lax.axis_size(axis))
    route = [(i - distance, i) for i in devices if i - distance in devices]
    return lax.ppermute(block, axis, route)


def normalize(values, norm_gain):
    return values * lax.rsqrt(jnp.mean(values * values, axis=-1, keepdims=True) + 1e-05) * norm_gain


def gated(normed, piece):
    gate_sum = jnp.dot(normed, piece[0], preferred_element_type=jnp.float32)
    upper_sum = jnp.dot(normed, piece[1], preferred_element_type=jnp.float32)
    return (jax.nn.silu(gate_sum) * upper_sum).astype(jnp.bfloat16)


def body(
    temporal,
    frame_ids,
    proj_weight,
    embed_table,
    qkv_weight,
    out_weight,
    gate_up,
    down_weight,
    norm_gains,
):
    code_index = lax.axis_index("codebook")
    hidden_index = lax.axis_index("hidden")
    hidden_count = lax.axis_size("hidden")
    start_id = embed_table.shape[1] - 1
    token_table = embed_table[0]
    norm_gain = norm_gains[0]
    earlier = shifted(frame_ids, "codebook", 1)[:, 0]
    previous = jnp.where(code_index == 0, start_id, earlier)
    partial_sum = jnp.dot(
        lax.all_gather(temporal, "codebook", axis=0, tiled=True),
        proj_weight[0],
        preferred_element_type=jnp.float32,
    )
    row_count = partial_sum.shape[0]
    x_zero = lax.psum(partial_sum.astype(jnp.bfloat16), "hidden").astype(jnp.float32) + token_table[
        previous
    ].astype(jnp.float32)
    normed = normalize(x_zero, norm_gain[0]).astype(jnp.bfloat16)
    local_width = qkv_weight.shape[3]
    local_heads = HEADS // hidden_count
    head_size = local_width // local_heads
    triple = jnp.einsum(
        "rd,kdc->krc", normed, qkv_weight[0], preferred_element_type=jnp.float32
    ).astype(jnp.bfloat16)
    query_heads = triple[0].reshape(row_count, local_heads, head_size)
    highest = jnp.full((row_count, local_heads), -1e30, jnp.float32)
    key_piece = lax.all_gather(triple[1][None], "codebook", axis=0, tiled=True)
    value_piece = lax.all_gather(triple[2][None], "codebook", axis=0, tiled=True)
    positions = key_piece.shape[0]
    key_heads = key_piece.reshape(positions, row_count, local_heads, head_size)
    value_heads = value_piece.reshape(positions, row_count, local_heads, head_size)
    scores = jnp.einsum(
        "fhd,jfhd->jfh", query_heads, key_heads, preferred_element_type=jnp.float32
    ) * head_size ** (-0.5)
    valid = (jnp.arange(positions, dtype=jnp.int32) <= code_index)[:, None, None]
    scores = jnp.where(valid, scores, -1e30)
    new_highest = jnp.maximum(highest, jnp.max(scores, axis=0))
    weights = jnp.where(valid, jnp.exp(scores - new_highest[None]), 0.0)
    running = jnp.sum(weights, axis=0)
    summed = jnp.einsum(
        "jfh,jfhd->fhd",
        weights.astype(jnp.bfloat16),
        value_heads,
        preferred_element_type=jnp.float32,
    )
    highest, running, summed = (new_highest, running, summed)
    attended = (summed / running[..., None]).reshape(row_count, local_width).astype(jnp.bfloat16)
    attention_part = jnp.dot(attended, out_weight[0], preferred_element_type=jnp.float32)
    residual = x_zero + lax.psum(attention_part.astype(jnp.bfloat16), "hidden").astype(jnp.float32)
    normed_two = normalize(residual, norm_gain[1]).astype(jnp.bfloat16)
    activated = gated(normed_two, gate_up[0])
    down_part = jnp.dot(activated, down_weight[0], preferred_element_type=jnp.float32)
    mlp_piece = lax.psum_scatter(
        down_part.astype(jnp.bfloat16), "hidden", scatter_dimension=1, tiled=True
    ).astype(jnp.float32)
    own_residual = lax.dynamic_slice_in_dim(residual, hidden_index * local_width, local_width, 1)
    return (own_residual + mlp_piece)[None]


def solution(mesh):
    placed = (
        P(("frames", "codebook"), "hidden"),
        P("frames", "codebook"),
        P("codebook", "hidden", None),
        P("codebook", None, None),
        P("codebook", None, None, "hidden"),
        P("codebook", "hidden", None),
        P("codebook", None, None, "hidden"),
        P("codebook", "hidden", None),
        P("codebook", None, None),
    )
    return jax.shard_map(
        body,
        mesh=mesh,
        in_specs=placed,
        out_specs=P("codebook", "frames", "hidden"),
        check_vma=False,
    )
```

profile of v0, /device:TPU:1, one launch (start us, length us, event | category | flops | bytes accessed | tf_op | source)
XLA Modules:
  0.0 563.1 jit_solution(17674491881883395552)
XLA Ops:
  6.5 0.0 copy-start
  6.5 0.7 all-gather.4.cloned.1.call-update
  7.3 0.0 all-reduce.3.cloned.1.call-start
  7.3 42.5 %all-gather.4.cloned.1.call-done = bf16[2048,1024]{1,0:T(8,128)(2,1)} async-done(((bf16[128,1024]{1,0:T(8,128)(2,1)}), bf16[2048,1024]{1,0:T(8,128)(2,1)}) %all-gather.4.cloned.1.call-update) | async-done | bytes 4194320 | tf_op jit(solution)/shard_map/all_gather | solution.py:45
  49.8 8.3 %convolution_convert_fusion.2 = bf16[2048,1024]{1,0:T(8,128)(2,1)} fusion(bf16[2048,1024]{1,0:T(8,128)(2,1)} %all-gather.4.cloned.1.call-done, bf16[1,1024,1024]{2,1,0:T(8,128)(2,1)S(1)} %copy-done), kind=kOutput, calls=%fused_computation.16 | convolution fusion | flops 4297064448 | bytes 10485760 | tf_op jit(solution)/shard_map/dot_general | solution.py:44
  58.2 0.0 all-reduce.3.cloned.1.call-update
  58.2 0.0 all-gather.6.cloned.1.call-start
  58.2 0.6 copy-done.9
  58.9 2.8 collective-permute-start
  61.7 0.0 copy-done.6
  61.8 0.7 collective-permute-done
  62.5 0.0 copy-start.8
  62.5 13.8 %gather_fusion = bf16[2048,1024]{1,0:T(8,128)(2,1)} fusion(bf16[2049,1024]{1,0:T(8,128)(2,1)} %bitcast.66, s32[2048]{0:T(1024)S(1)} %broadcast_clamp_fusion), kind=kCustom, calls=%fused_computation | custom fusion | bytes 8396800 | tf_op jit(solution)/shard_map/gather | solution.py:50
  76.3 74.6 %all-reduce.3.cloned.1.call-done = bf16[2048,1024]{1,0:T(8,128)(2,1)} async-done(((bf16[2048,1024]{1,0:T(8,128)(2,1)}), bf16[2048,1024]{1,0:T(8,128)(2,1)}) %all-reduce.3.cloned.1.call-update) | async-done | bytes 4194320 | tf_op jit(solution)/shard_map/psum | solution.py:50
  150.9 5.0 multiply_reduce_fusion.3
  155.9 0.0 copy-done.8
  156.0 0.0 copy-done.2
  156.0 0.9 copy-done.3
  156.8 4.2 fusion.8
  161.0 0.3 fusion.30
  161.3 1.3 copy.21
  162.7 0.0 all-gather.6.cloned.1.call-update
  162.7 0.0 all-gather.8.cloned.1.call-start
  162.7 1.3 copy.23
  164.1 0.0 all-gather.8.cloned.1.call-update
  164.1 0.2 all-reduce.5.cloned.1.call-start
  164.3 0.2 convert.1
  164.6 90.1 %all-gather.6.cloned.1.call-done = bf16[16,2048,256]{2,1,0:T(8,128)(2,1)} async-done(((bf16[1,2048,256]{2,1,0:T(8,128)(2,1)}), bf16[16,2048,256]{2,1,0:T(8,128)(2,1)}) %all-gather.6.cloned.1.call-update) | async-done | bytes 16777232 | tf_op jit(solution)/shard_map/all_gather | solution.py:62
  254.7 22.0 %copy.40 = bf16[16,2048,256]{1,2,0:T(8,128)(2,1)} copy(bf16[16,2048,256]{2,1,0:T(8,128)(2,1)} %all-gather.6.cloned.1.call-done) | data formatting | bytes 33554432
  276.7 7.9 %multiply_reduce_fusion.1 = f32[2048,4,16]{0,1,2:T(4,128)S(1)} fusion(f32[2048,4,64]{0,2,1:T(8,128)S(1)} %convert.1, bf16[16,2048,256]{1,2,0:T(8,128)(2,1)} %copy.40), kind=kLoop, calls=%fused_computation.2 | loop fusion | flops 25034752 | bytes 19398656
  284.5 0.4 bitcast_reduce_fusion
  284.9 0.5 fusion.25
  285.4 0.3 copy.43
  285.8 62.8 %all-gather.8.cloned.1.call-done = bf16[16,2048,256]{2,1,0:T(8,128)(2,1)} async-done(((bf16[1,2048,256]{2,1,0:T(8,128)(2,1)}), bf16[16,2048,256]{2,1,0:T(8,128)(2,1)}) %all-gather.8.cloned.1.call-update) | async-done | bytes 16777232 | tf_op jit(solution)/shard_map/all_gather | solution.py:63
  348.6 21.7 %copy.41 = bf16[16,2048,256]{1,2,0:T(8,128)(2,1)} copy(bf16[16,2048,256]{2,1,0:T(8,128)(2,1)} %all-gather.8.cloned.1.call-done) | data formatting | bytes 33554432
  370.3 7.7 %multiply_reduce_fusion = f32[2048,4,64]{0,2,1:T(8,128)S(1)} fusion(bf16[2048,4,16,64]{0,3,1,2:T(8,128)(2,1)} %bitcast.67, f32[2048,4,16]{0,1,2:T(4,128)S(1)} %copy.43), kind=kLoop, calls=%fused_computation.1 | loop fusion | flops 24641536 | bytes 19398656 | tf_op jit(solution)/shard_map/jfh,jfhd->fhd/dot_general | solution.py:75
  377.9 0.2 divide_convert_fusion
  378.1 3.3 convolution_convert_fusion
  381.4 0.0 all-reduce.5.cloned.1.call-update
  381.4 0.0 reduce-scatter.2.cloned.1.call-start
  381.5 93.4 %all-reduce.5.cloned.1.call-done = bf16[2048,1024]{1,0:T(8,128)(2,1)} async-done(((bf16[2048,1024]{1,0:T(8,128)(2,1)}), bf16[2048,1024]{1,0:T(8,128)(2,1)}) %all-reduce.5.cloned.1.call-update) | async-done | bytes 4194320 | tf_op jit(solution)/shard_map/psum | solution.py:84
  474.9 5.8 %multiply_reduce_fusion.2 = (f32[2048]{0:T(1024)S(1)}, f32[2048,1024]{1,0:T(8,128)S(1)}) fusion(bf16[2048,1024]{1,0:T(8,128)(2,1)} %all-reduce.5.cloned.1.call-done, bf16[2048,1024]{1,0:T(8,128)(2,1)} %gather_fusion, bf16[2048,1024]{1,0:T(8,128)(2,1)} %all-reduce.3.cloned.1.call-done), kind=kLoop, calls=%fused_computation.5 | loop fusion | flops 14678016 | bytes 20979712 | tf_op jit(solution)/shard_map/reduce_sum | solution.py:16
  480.7 3.2 copy-done.4
  483.9 6.7 %fusion.14 = f32[2048,1024]{1,0:T(8,128)} fusion(bf16[1,2,1024,1024]{3,2,1,0:T(8,128)(2,1)S(1)} %copy-done.7, f32[2048,1024]{1,0:T(8,128)S(1)} %get-tuple-element.6, f32[1024]{0:T(1024)S(1)} %bitcast.71, f32[2048]{0:T(1024)S(1)} %add_rsqrt_fusion), kind=kOutput, calls=%fused_computation.21 | convolution fusion | flops 4301258752 | bytes 18886656 | tf_op jit(solution)/shard_map/dot_general | solution.py:20
  490.6 15.1 %convolution_convert_fusion.1 = bf16[2048,1024]{1,0:T(8,128)(2,1)} fusion(f32[2048,1024]{1,0:T(8,128)} %fusion.14, bf16[1,1024,1024]{2,1,0:T(8,128)(2,1)} %param.16, bf16[1,2,1024,1024]{3,2,1,0:T(8,128)(2,1)} %param.15, f32[2048,1024]{1,0:T(8,128)} %copy-done.4, f32[1024]{0:T(1024)S(1)} %bitcast.72, f32[2048]{0:T(1024)S(1)} %add_rsqrt_fusion), kind=kOutput, calls=%fused_computation.15 | convolution fusion | flops 8610906112 | bytes 25178112 | tf_op jit(solution)/shard_map/dot_general | solution.py:87
  505.8 0.0 reduce-scatter.2.cloned.1.call-update
  505.8 47.0 %reduce-scatter.2.cloned.1.call-done = bf16[2048,256]{1,0:T(8,128)(2,1)} async-done(((bf16[2048,1024]{1,0:T(8,128)(2,1)}), bf16[2048,256]{1,0:T(8,128)(2,1)}) %reduce-scatter.2.cloned.1.call-update) | async-done | bytes 1048592 | tf_op jit(solution)/shard_map/reduce_scatter | solution.py:88
  552.9 3.4 add_bitcast_fusion
  (20 shorter events, 0.1 us)
Async XLA Ops:
  6.5 43.3 %copy-start = (bf16[1,1024,1024]{2,1,0:T(8,128)(2,1)S(1)}, bf16[1,1024,1024]{2,1,0:T(8,128)(2,1)}, u32[]{:S(2)}) copy-start(bf16[1,1024,1024]{2,1,0:T(8,128)(2,1)} %param.11) | copy-start | bytes 6291460
  6.5 43.3 %all-gather.4.cloned.1.call-start = ((), (), s32[]{:S(2)}) async-start(), calls=%async_computation.1 | async-start | bytes 4456448 | tf_op jit(solution)/shard_map/all_gather | solution.py:45
  7.3 143.6 %all-reduce.3.cloned.1.call-start = ((), (), s32[]{:S(2)}) async-start(), calls=%async_computation.2 | async-start | bytes 8388608 | tf_op jit(solution)/shard_map/psum | solution.py:50
  58.2 0.7 copy-start.9
  58.2 3.5 copy-start.6
  58.2 196.5 %all-gather.6.cloned.1.call-start = ((), (), s32[]{:S(2)}) async-start(), calls=%async_computation.3 | async-start | bytes 17825792 | tf_op jit(solution)/shard_map/all_gather | solution.py:62
  58.9 3.6 collective-permute-start
  62.5 93.4 %copy-start.8 = (bf16[1,3,1024,256]{3,2,1,0:T(8,128)(2,1)S(1)}, bf16[1,3,1024,256]{3,2,1,0:T(8,128)(2,1)}, u32[]{:S(2)}) copy-start(bf16[1,3,1024,256]{3,2,1,0:T(8,128)(2,1)} %param.13) | copy-start | bytes 4718596
  150.9 5.1 copy-start.2
  150.9 5.9 %copy-start.3 = (bf16[2048,1024]{1,0:T(8,128)(2,1)S(1)}, bf16[2048,1024]{1,0:T(8,128)(2,1)}, u32[]{:S(2)}) copy-start(bf16[2048,1024]{1,0:T(8,128)(2,1)} %all-reduce.3.cloned.1.call-done) | copy-start | bytes 12582916
  162.7 185.9 %all-gather.8.cloned.1.call-start = ((), (), s32[]{:S(2)}) async-start(), calls=%async_computation.4 | async-start | bytes 17825792 | tf_op jit(solution)/shard_map/all_gather | solution.py:63
  164.1 310.8 %all-reduce.5.cloned.1.call-start = ((), (), s32[]{:S(2)}) async-start(), calls=%async_computation.5 | async-start | bytes 8388608 | tf_op jit(solution)/shard_map/psum | solution.py:84
  370.3 7.9 %copy-start.5 = (bf16[1,256,1024]{2,1,0:T(8,128)(2,1)S(1)}, bf16[1,256,1024]{2,1,0:T(8,128)(2,1)}, u32[]{:S(2)}) copy-start(bf16[1,256,1024]{2,1,0:T(8,128)(2,1)} %param.14) | copy-start | bytes 1572868
  381.4 171.4 %reduce-scatter.2.cloned.1.call-start = ((), (), s32[]{:S(2)}) async-start(), calls=%async_computation.6 | async-start | bytes 5242880 | tf_op jit(solution)/shard_map/reduce_scatter | solution.py:88
  474.9 9.1 %copy-start.7 = (bf16[1,2,1024,1024]{3,2,1,0:T(8,128)(2,1)S(1)}, bf16[1,2,1024,1024]{3,2,1,0:T(8,128)(2,1)}, u32[]{:S(2)}) copy-start(bf16[1,2,1024,1024]{3,2,1,0:T(8,128)(2,1)} %param.15) | copy-start | bytes 12582916
  480.7 3.2 copy-start.4
  505.8 50.5 %copy-start.1 = (bf16[1,1024,1024]{2,1,0:T(8,128)(2,1)S(1)}, bf16[1,1024,1024]{2,1,0:T(8,128)(2,1)}, u32[]{:S(2)}) copy-start(bf16[1,1024,1024]{2,1,0:T(8,128)(2,1)} %param.11) | copy-start | bytes 6291460
Sparse Core Ops, SparseCore 0:
  9.0 40.7 all-gather.3
  58.3 92.5 all-reduce.2
  162.8 91.8 all-gather.5
  256.2 92.3 all-gather.7
  381.6 93.2 all-reduce.4
  505.9 46.8 reduce-scatter.1
where the time goes:
time: 564 us; the launch traced here: 563 us
  waiting for transfers between devices  412 us (73%)
  local copies, waits for them, and re-layouts  65.5 us (12%)
  matrix products  37.6 us (7%)
  other arithmetic  31.1 us (6%)
  between operations  13.7 us (2%)
    psum x1, waiting for transfers between devices, body(): lax.psum(attention_part.astype(jnp.bfloat16), 'hidden').astype(jnp.float32)  93.4 us
    all_gather x1, waiting for transfers between devices, body(): key_piece = lax.all_gather(triple[1][None], 'codebook', axis=0, tiled=True)  90.1 us
    psum x1, waiting for transfers between devices, body(): lax.psum(partial_sum.astype(jnp.bfloat16), 'hidden').astype(jnp.float32)  74.6 us
    all_gather x1, waiting for transfers between devices, body(): lax.all_gather(triple[2][None], 'codebook', axis=0, tiled=True)  62.8 us
    unnamed x23, local copies, waits for them, and re-layouts  48.7 us
    reduce_scatter x1, waiting for transfers between devices, body(): lax.psum_scatter(down_part.astype(jnp.bfloat16), 'hidden', scatter_dimens...  47 us
    all_gather x1, waiting for transfers between devices, body(): lax.all_gather(temporal, 'codebook', axis=0, tiled=True)  42.5 us
    dot_general x1, matrix products, body(): jnp.dot(activated, down_weight[0], preferred_element_type=jnp.float32)  15.1 us
  transfers between devices with their start and end apart: 7, of which 7 were waited for; matrix products, arithmetic and copies ran while one was open for 8% of the time, Pallas kernels for 0%

commit v1 on v0

--- a/solution.py
+++ b/solution.py
@@ -4,6 +4,13 @@
 from jax.sharding import PartitionSpec as P
 
 HEADS = 16
+
+
+def gather_over(block, axis, along):
+    size = lax.axis_size(axis)
+    parts = jnp.stack([block for _ in range(size)])
+    parts = lax.all_to_all(parts, axis, split_axis=0, concat_axis=0)
+    return jnp.concatenate(parts, axis=along)
 
 
 def shifted(block, axis, distance):
@@ -42,9 +49,7 @@
     earlier = shifted(frame_ids, "codebook", 1)[:, 0]
     previous = jnp.where(code_index == 0, start_id, earlier)
     partial_sum = jnp.dot(
-        lax.all_gather(temporal, "codebook", axis=0, tiled=True),
-        proj_weight[0],
-        preferred_element_type=jnp.float32,
+        gather_over(temporal, "codebook", 0), proj_weight[0], preferred_element_type=jnp.float32
     )
     row_count = partial_sum.shape[0]
     x_zero = lax.psum(partial_sum.astype(jnp.bfloat16), "hidden").astype(jnp.float32) + token_table[

time: 564 us -> 576 us (1.021)
  blocking collectives: 0 us -> 55.4 us
  waiting for transfers between devices: 412 us -> 371 us
    all_to_all x0 -> x1, blocking collectives: none -> 55.4 us  [gather_over(): parts = lax.all_to_all(parts, axis, split_axis=0, concat_axis=0)]
    all_gather x1 -> x0, waiting for transfers between devices: 42.5 us -> none  [body(): lax.all_gather(temporal, 'codebook', axis=0, tiled=True)]
  transfers between devices with their start and end apart: 7 -> 6, of which waited for: 7 -> 6; matrix products, arithmetic and copies ran while one was open for 8% -> 8% of each run, Pallas kernels for 0% -> 0%
where the time goes in v1:
time: 576 us; the launch traced here: 575 us
  waiting for transfers between devices  371 us (64%)
  local copies, waits for them, and re-layouts  67.2 us (12%)
  blocking collectives  55.4 us (10%)
  matrix products  35.3 us (6%)
  other arithmetic  31.1 us (5%)
  between operations  13.3 us (2%)
    psum x1, waiting for transfers between devices, body(): lax.psum(attention_part.astype(jnp.bfloat16), 'hidden').astype(jnp.float32)  93.4 us
    all_gather x1, waiting for transfers between devices, body(): key_piece = lax.all_gather(triple[1][None], 'codebook', axis=0, tiled=True)  90.1 us
    psum x1, waiting for transfers between devices, body(): lax.psum(partial_sum.astype(jnp.bfloat16), 'hidden').astype(jnp.float32)  75.6 us
    all_gather x1, waiting for transfers between devices, body(): lax.all_gather(triple[2][None], 'codebook', axis=0, tiled=True)  62.9 us
    all_to_all x1, blocking collectives, gather_over(): parts = lax.all_to_all(parts, axis, split_axis=0, concat_axis=0)  55.4 us
    unnamed x23, local copies, waits for them, and re-layouts  48.8 us
    reduce_scatter x1, waiting for transfers between devices, body(): lax.psum_scatter(down_part.astype(jnp.bfloat16), 'hidden', scatter_dimens...  47 us
    dot_general x1, matrix products, body(): jnp.dot(activated, down_weight[0], preferred_element_type=jnp.float32)  15.1 us
  transfers between devices with their start and end apart: 6, of which 6 were waited for; matrix products, arithmetic and copies ran while one was open for 8% of the time, Pallas kernels for 0%

profile of v1, /device:TPU:1, one launch (start us, length us, event | category | flops | bytes accessed | tf_op | source)
XLA Modules:
  0.0 575.1 jit_solution(14632051651494889656)
XLA Ops:
  6.5 0.0 copy-start
  6.5 0.0 all-reduce.3.cloned.1.call-start
  6.5 1.6 stack.2
  8.2 55.4 %all_to_all.5 = bf16[16,128,1024]{2,1,0:T(8,128)(2,1)S(1)} all-to-all(bf16[16,128,1024]{2,1,0:T(8,128)(2,1)S(1)} %stack.2), channel_id=1, replica_groups=mesh['frames'=2,'codebook'=16,'hidden'=4] {'codebook'}, dimensions={0} | all-to-all | bytes 8388608 | tf_op jit(solution)/shard_map/all_to_all | solution.py:12
  63.6 0.0 copy-done
  63.6 6.0 %convolution_convert_fusion.2 = bf16[2048,1024]{1,0:T(8,128)(2,1)} fusion(bf16[2048,1024]{1,0:T(8,128)(2,1)S(1)} %bitcast.70, bf16[1,1024,1024]{2,1,0:T(8,128)(2,1)S(1)} %copy-done), kind=kOutput, calls=%fused_computation.16 | convolution fusion | flops 4297064448 | bytes 10485760 | tf_op jit(solution)/shard_map/dot_general | solution.py:51
  69.6 0.0 all-reduce.3.cloned.1.call-update
  69.6 0.0 all-gather.3.cloned.1.call-start
  69.7 0.6 copy-done.9
  70.3 1.9 collective-permute-start
  72.2 1.4 collective-permute-done
  73.7 0.0 copy-start.8
  73.7 13.8 %gather_fusion = bf16[2048,1024]{1,0:T(8,128)(2,1)} fusion(bf16[2049,1024]{1,0:T(8,128)(2,1)} %bitcast.67, s32[2048]{0:T(1024)S(1)} %broadcast_clamp_fusion), kind=kCustom, calls=%fused_computation | custom fusion | bytes 8396800 | tf_op jit(solution)/shard_map/gather | solution.py:55
  87.5 75.6 %all-reduce.3.cloned.1.call-done = bf16[2048,1024]{1,0:T(8,128)(2,1)} async-done(((bf16[2048,1024]{1,0:T(8,128)(2,1)}), bf16[2048,1024]{1,0:T(8,128)(2,1)}) %all-reduce.3.cloned.1.call-update) | async-done | bytes 4194320 | tf_op jit(solution)/shard_map/psum | solution.py:55
  163.1 5.0 multiply_reduce_fusion.3
  168.1 0.9 copy-done.3
  169.0 4.2 fusion.8
  173.2 0.3 fusion.30
  173.5 1.3 copy.21
  174.8 0.0 all-gather.3.cloned.1.call-update
  174.8 0.0 all-gather.5.cloned.1.call-start
  174.9 1.3 copy.23
  176.2 0.0 all-gather.5.cloned.1.call-update
  176.2 0.2 all-reduce.5.cloned.1.call-start
  176.5 0.2 convert.1
  176.7 90.1 %all-gather.3.cloned.1.call-done = bf16[16,2048,256]{2,1,0:T(8,128)(2,1)} async-done(((bf16[1,2048,256]{2,1,0:T(8,128)(2,1)}), bf16[16,2048,256]{2,1,0:T(8,128)(2,1)}) %all-gather.3.cloned.1.call-update) | async-done | bytes 16777232 | tf_op jit(solution)/shard_map/all_gather | solution.py:67
  266.8 22.1 %copy.40 = bf16[16,2048,256]{1,2,0:T(8,128)(2,1)} copy(bf16[16,2048,256]{2,1,0:T(8,128)(2,1)} %all-gather.3.cloned.1.call-done) | data formatting | bytes 33554432
  288.9 7.9 %multiply_reduce_fusion.1 = f32[2048,4,16]{0,1,2:T(4,128)S(1)} fusion(f32[2048,4,64]{0,2,1:T(8,128)S(1)} %convert.1, bf16[16,2048,256]{1,2,0:T(8,128)(2,1)} %copy.40), kind=kLoop, calls=%fused_computation.2 | loop fusion | flops 25034752 | bytes 19398656
  296.7 0.4 bitcast_reduce_fusion
  297.1 0.5 fusion.25
  297.6 0.3 copy.43
  298.0 62.9 %all-gather.5.cloned.1.call-done = bf16[16,2048,256]{2,1,0:T(8,128)(2,1)} async-done(((bf16[1,2048,256]{2,1,0:T(8,128)(2,1)}), bf16[16,2048,256]{2,1,0:T(8,128)(2,1)}) %all-gather.5.cloned.1.call-update) | async-done | bytes 16777232 | tf_op jit(solution)/shard_map/all_gather | solution.py:68
  360.9 21.7 %copy.41 = bf16[16,2048,256]{1,2,0:T(8,128)(2,1)} copy(bf16[16,2048,256]{2,1,0:T(8,128)(2,1)} %all-gather.5.cloned.1.call-done) | data formatting | bytes 33554432
  382.6 7.7 %multiply_reduce_fusion = f32[2048,4,64]{0,2,1:T(8,128)S(1)} fusion(bf16[2048,4,16,64]{0,3,1,2:T(8,128)(2,1)} %bitcast.68, f32[2048,4,16]{0,1,2:T(4,128)S(1)} %copy.43), kind=kLoop, calls=%fused_computation.1 | loop fusion | flops 24641536 | bytes 19398656 | tf_op jit(solution)/shard_map/jfh,jfhd->fhd/dot_general | solution.py:80
  390.3 0.2 divide_convert_fusion
  390.5 3.3 convolution_convert_fusion
  393.7 0.0 all-reduce.5.cloned.1.call-update
  393.7 0.0 reduce-scatter.2.cloned.1.call-start
  393.8 93.4 %all-reduce.5.cloned.1.call-done = bf16[2048,1024]{1,0:T(8,128)(2,1)} async-done(((bf16[2048,1024]{1,0:T(8,128)(2,1)}), bf16[2048,1024]{1,0:T(8,128)(2,1)}) %all-reduce.5.cloned.1.call-update) | async-done | bytes 4194320 | tf_op jit(solution)/shard_map/psum | solution.py:89
  487.2 5.8 %multiply_reduce_fusion.2 = (f32[2048]{0:T(1024)S(1)}, f32[2048,1024]{1,0:T(8,128)S(1)}) fusion(bf16[2048,1024]{1,0:T(8,128)(2,1)} %all-reduce.5.cloned.1.call-done, bf16[2048,1024]{1,0:T(8,128)(2,1)} %gather_fusion, bf16[2048,1024]{1,0:T(8,128)(2,1)} %all-reduce.3.cloned.1.call-done), kind=kLoop, calls=%fused_computation.5 | loop fusion | flops 14678016 | bytes 20979712 | tf_op jit(solution)/shard_map/reduce_sum | solution.py:23
  493.0 0.0 copy-start.4
  493.0 3.2 copy-done.4
  496.2 0.0 copy-done.7
  496.2 6.7 %fusion.14 = f32[2048,1024]{1,0:T(8,128)} fusion(bf16[1,2,1024,1024]{3,2,1,0:T(8,128)(2,1)S(1)} %copy-done.7, f32[2048,1024]{1,0:T(8,128)S(1)} %get-tuple-element.6, f32[1024]{0:T(1024)S(1)} %bitcast.73, f32[2048]{0:T(1024)S(1)} %add_rsqrt_fusion), kind=kOutput, calls=%fused_computation.21 | convolution fusion | flops 4301258752 | bytes 18886656 | tf_op jit(solution)/shard_map/dot_general | solution.py:27
  503.0 15.1 %convolution_convert_fusion.1 = bf16[2048,1024]{1,0:T(8,128)(2,1)} fusion(f32[2048,1024]{1,0:T(8,128)} %fusion.14, bf16[1,1024,1024]{2,1,0:T(8,128)(2,1)} %param.16, bf16[1,2,1024,1024]{3,2,1,0:T(8,128)(2,1)} %param.15, f32[2048,1024]{1,0:T(8,128)} %copy-done.4, f32[1024]{0:T(1024)S(1)} %bitcast.74, f32[2048]{0:T(1024)S(1)} %add_rsqrt_fusion), kind=kOutput, calls=%fused_computation.15 | convolution fusion | flops 8610906112 | bytes 25178112 | tf_op jit(solution)/shard_map/dot_general | solution.py:92
  518.1 0.0 reduce-scatter.2.cloned.1.call-update
  518.1 47.0 %reduce-scatter.2.cloned.1.call-done = bf16[2048,256]{1,0:T(8,128)(2,1)} async-done(((bf16[2048,1024]{1,0:T(8,128)(2,1)}), bf16[2048,256]{1,0:T(8,128)(2,1)}) %reduce-scatter.2.cloned.1.call-update) | async-done | bytes 1048592 | tf_op jit(solution)/shard_map/reduce_scatter | solution.py:93
  565.2 3.4 add_bitcast_fusion
  (19 shorter events, 0.1 us)
Async XLA Ops:
  6.5 57.1 %copy-start = (bf16[1,1024,1024]{2,1,0:T(8,128)(2,1)S(1)}, bf16[1,1024,1024]{2,1,0:T(8,128)(2,1)}, u32[]{:S(2)}) copy-start(bf16[1,1024,1024]{2,1,0:T(8,128)(2,1)} %param.11) | copy-start | bytes 6291460
  6.5 156.5 %all-reduce.3.cloned.1.call-start = ((), (), s32[]{:S(2)}) async-start(), calls=%async_computation.2 | async-start | bytes 8388608 | tf_op jit(solution)/shard_map/psum | solution.py:55
  69.6 0.7 copy-start.9
  69.6 2.6 copy-start.6
  69.6 197.2 %all-gather.3.cloned.1.call-start = ((), (), s32[]{:S(2)}) async-start(), calls=%async_computation.3 | async-start | bytes 17825792 | tf_op jit(solution)/shard_map/all_gather | solution.py:67
  70.3 3.4 collective-permute-start
  73.7 94.4 %copy-start.8 = (bf16[1,3,1024,256]{3,2,1,0:T(8,128)(2,1)S(1)}, bf16[1,3,1024,256]{3,2,1,0:T(8,128)(2,1)}, u32[]{:S(2)}) copy-start(bf16[1,3,1024,256]{3,2,1,0:T(8,128)(2,1)} %param.13) | copy-start | bytes 4718596
  163.1 5.1 copy-start.2
  163.1 5.9 %copy-start.3 = (bf16[2048,1024]{1,0:T(8,128)(2,1)S(1)}, bf16[2048,1024]{1,0:T(8,128)(2,1)}, u32[]{:S(2)}) copy-start(bf16[2048,1024]{1,0:T(8,128)(2,1)} %all-reduce.3.cloned.1.call-done) | copy-start | bytes 12582916
  174.8 186.0 %all-gather.5.cloned.1.call-start = ((), (), s32[]{:S(2)}) async-start(), calls=%async_computation.4 | async-start | bytes 17825792 | tf_op jit(solution)/shard_map/all_gather | solution.py:68
  176.2 310.9 %all-reduce.5.cloned.1.call-start = ((), (), s32[]{:S(2)}) async-start(), calls=%async_computation.5 | async-start | bytes 8388608 | tf_op jit(solution)/shard_map/psum | solution.py:89
  382.6 7.9 %copy-start.5 = (bf16[1,256,1024]{2,1,0:T(8,128)(2,1)S(1)}, bf16[1,256,1024]{2,1,0:T(8,128)(2,1)}, u32[]{:S(2)}) copy-start(bf16[1,256,1024]{2,1,0:T(8,128)(2,1)} %param.14) | copy-start | bytes 1572868
  393.7 171.4 %reduce-scatter.2.cloned.1.call-start = ((), (), s32[]{:S(2)}) async-start(), calls=%async_computation.6 | async-start | bytes 5242880 | tf_op jit(solution)/shard_map/reduce_scatter | solution.py:93
  487.2 9.1 %copy-start.7 = (bf16[1,2,1024,1024]{3,2,1,0:T(8,128)(2,1)S(1)}, bf16[1,2,1024,1024]{3,2,1,0:T(8,128)(2,1)}, u32[]{:S(2)}) copy-start(bf16[1,2,1024,1024]{3,2,1,0:T(8,128)(2,1)} %param.15) | copy-start | bytes 12582916
  493.0 3.2 copy-start.4
  518.1 50.5 %copy-start.1 = (bf16[1,1024,1024]{2,1,0:T(8,128)(2,1)S(1)}, bf16[1,1024,1024]{2,1,0:T(8,128)(2,1)}, u32[]{:S(2)}) copy-start(bf16[1,1024,1024]{2,1,0:T(8,128)(2,1)} %param.11) | copy-start | bytes 6291460
Sparse Core Ops, SparseCore 0:
  69.7 93.2 all-reduce.2
  175.0 91.8 all-gather.2
  268.5 92.3 all-gather.4
  393.9 93.2 all-reduce.4
  518.2 46.8 reduce-scatter.1
